TPU v7x, 32 devices: a whole 2x2x4 slice. The times are simulated.
32 devices in a mesh: gx: 4 (over y, core), gy: 8 (over z, x).
Axes of the slice: x: 2, y: 2, z: 4, core: 2. Of those that a mesh axis runs over, the one named last changes fastest.
Arguments:
- velocity: float32 [3, 32, 64, 128], P(None, 'gx', 'gy'), may hold values from -2 to 2
- pressure: float32 [32, 64, 128], P('gx', 'gy'), may hold values from -6 to 6
- buoyancy: float32 [32, 64, 128], P('gx', 'gy'), may hold values from -6 to 6
- background: float32 [32, 64, 128], P('gx', 'gy'), may hold values from -0.7 to 0.7
- marker_value: float32 [8192, 256], P(('gx', 'gy')), may hold values from -2.5 to 2.5
- marker_height: float32 [8192, 256], P(('gx', 'gy')), may hold values from 0 to 127
- marker_owner: int32 [8192, 1], P(('gx', 'gy')), may hold values from 0 to 31; in each aligned block of 256 rows (0 to 255, 256 to 511, ...) at most 16 rows name the same one
- marker_column: int32 [8192], P(('gx', 'gy')), may hold values from 0 to 63
- block_count: int32 [32], P(('gx', 'gy')), may hold values from 1 to 256, 6144 in all
Outputs:
- new_velocity: float32 [3, 32, 64, 128], P(None, 'gx', 'gy')
- new_pressure: float32 [32, 64, 128], P('gx', 'gy')
- viscosity: float32 [32, 64, 128], P('gx', 'gy')
Inputs may be any that keep to these rules, and one draw needn't show every extreme that they name: `marker_owner`: among the 256 blocks of one device at most 16 name the same owner, and for some owner exactly 16 do. A device's live blocks are its first block_count ones; some device has all 256 live.
All inputs are finite; a program needn't handle non-finite values.
Results may differ from a plain program's by a relative error of at most 0.0003.
Values sent between devices are 32-bit elements; how exact they have to be, the bound alone decides.
No kernel may reach another device: no remote copies, remote signals or barrier semaphores. Data moves between devices by JAX's collectives and lax.ppermute only.
A program may use at most 64 MiB of HBM per device.

v0:
```python
import jax
import jax.numpy as jnp
from jax import lax
from jax.sharding import PartitionSpec as P

ITERS = 2
PRESS_STEP = 0.5
VEL_STEP = 0.05
DAMPING = 0.8


def extended(x, sides, width):
    for axis, dim in sides:
        devices, length = (lax.axis_size(axis), x.shape[dim])
        up = [(i, (i + 1) % devices) for i in range(devices - 1)]
        down = [(j, i) for i, j in up]
        last = lax.slice_in_dim(x, length - width, length, axis=dim)
        first = lax.slice_in_dim(x, 0, width, axis=dim)
        before = lax.ppermute(last, axis, up)
        after = lax.ppermute(first, axis, down)
        x = jnp.concatenate([before, x, after], axis=dim)
    return x


def inner_of(field):
    return field[..., 1:-1, 1:-1, :]


def east_of(field):
    return field[..., 2:, 1:-1, :]


def west_of(field):
    return field[..., :-2, 1:-1, :]


def north_of(field):
    return field[..., 1:-1, 2:, :]


def south_of(field):
    return field[..., 1:-1, :-2, :]


def upper_of(field):
    return jnp.concatenate([field[..., 1:], jnp.zeros_like(field[..., :1])], axis=-1)


def lower_of(field):
    return jnp.concatenate([jnp.zeros_like(field[..., :1]), field[..., :-1]], axis=-1)


def column_profile(values, heights, num_levels):
    lower_f = jnp.minimum(jnp.floor(heights), num_levels - 2.0)
    fraction = heights - lower_f
    lower_idx = lower_f.astype(jnp.int32)
    levels = jnp.arange(num_levels, dtype=jnp.int32)
    at_low = lower_idx[..., None] == levels
    at_up = (lower_idx + 1)[..., None] == levels
    weight = jnp.where(at_low, (1.0 - fraction)[..., None], 0.0) + jnp.where(
        at_up, fraction[..., None], 0.0
    )
    value_sum = jnp.sum(weight * values[..., None], axis=1)
    weight_sum = jnp.sum(weight, axis=1)
    return jnp.stack([value_sum, weight_sum], axis=1)


def place_rows(rows, profile, total_rows):
    one_hot = (jnp.arange(total_rows, dtype=jnp.int32)[:, None] == rows[None, :]).astype(
        jnp.float32
    )
    flat = profile.reshape(profile.shape[0], -1)
    return jnp.dot(
        one_hot, flat, precision=lax.Precision.HIGHEST, preferred_element_type=jnp.float32
    )


def stresses(vel_pad, visc_pad, pressure):
    vel_x = inner_of(vel_pad[0])
    vel_y = inner_of(vel_pad[1])
    vel_z = inner_of(vel_pad[2])
    visc = inner_of(visc_pad)
    grad_xx = vel_x - west_of(vel_pad[0])
    grad_yy = vel_y - south_of(vel_pad[1])
    grad_zz = vel_z - lower_of(vel_z)
    divergence = grad_xx + grad_yy + grad_zz
    new_press = pressure - PRESS_STEP * visc * divergence
    third = divergence / 3.0
    sig_xx = 2.0 * visc * (grad_xx - third) - new_press
    sig_yy = 2.0 * visc * (grad_yy - third) - new_press
    sig_zz = 2.0 * visc * (grad_zz - third) - new_press
    corner_xy = 0.25 * (visc + east_of(visc_pad) + north_of(visc_pad) + visc_pad[..., 2:, 2:, :])
    side_x = visc + east_of(visc_pad)
    side_y = visc + north_of(visc_pad)
    corner_xz = 0.25 * (side_x + upper_of(side_x))
    corner_yz = 0.25 * (side_y + upper_of(side_y))
    tau_xy = corner_xy * (north_of(vel_pad[0]) - vel_x + east_of(vel_pad[1]) - vel_y)
    tau_xz = corner_xz * (upper_of(vel_x) - vel_x + east_of(vel_pad[2]) - vel_z)
    tau_yz = corner_yz * (upper_of(vel_y) - vel_y + north_of(vel_pad[2]) - vel_z)
    return (new_press, jnp.stack([sig_xx, sig_yy, tau_xy, tau_xz, tau_yz]), sig_zz)


def residuals(stress_pad, sig_zz, buoyancy):
    sig_xx = stress_pad[0]
    sig_yy = stress_pad[1]
    tau_xy = stress_pad[2]
    tau_xz = stress_pad[3]
    tau_yz = stress_pad[4]
    mid_xz = inner_of(tau_xz)
    mid_yz = inner_of(tau_yz)
    res_x = (
        east_of(sig_xx)
        - inner_of(sig_xx)
        + inner_of(tau_xy)
        - south_of(tau_xy)
        + mid_xz
        - lower_of(mid_xz)
    )
    res_y = (
        inner_of(tau_xy)
        - west_of(tau_xy)
        + north_of(sig_yy)
        - inner_of(sig_yy)
        + mid_yz
        - lower_of(mid_yz)
    )
    res_z = (
        mid_xz - west_of(tau_xz) + mid_yz - south_of(tau_yz) + upper_of(sig_zz) - sig_zz + buoyancy
    )
    return jnp.stack([res_x, res_y, res_z])


def advance(vel, moment, residual, visc_pad, masks):
    visc = inner_of(visc_pad)
    faces = jnp.stack(
        [
            0.5 * (visc + east_of(visc_pad)),
            0.5 * (visc + north_of(visc_pad)),
            0.5 * (visc + upper_of(visc)),
        ]
    )
    moment = DAMPING * moment + residual
    vel = masks * (vel + VEL_STEP * moment / faces)
    return (vel, moment)


def rims(field):
    return extended(field, (("gx", 1), ("gy", 2)), 1)


def shards(
    velocity,
    pressure,
    buoyancy,
    background,
    marker_value,
    marker_height,
    marker_owner,
    marker_column,
    block_count,
):
    cells_x, cells_y, num_levels = pressure.shape
    block_rows = marker_owner.shape[0]
    size_x = lax.axis_size("gx")
    size_y = lax.axis_size("gy")
    devices = size_x * size_y
    capacity = max(2, (2 * block_rows + devices - 1) // devices)
    columns_n = cells_x * cells_y
    owner = marker_owner[:, 0]
    live = jnp.arange(block_rows) < block_count[0]
    hits = ((owner[:, None] == jnp.arange(devices)[None, :]) & live[:, None]).astype(jnp.int32)
    ranks = jnp.sum((jnp.cumsum(hits, axis=0) - 1) * hits, axis=1)
    slots = jnp.where(live, owner * capacity + ranks, devices * capacity)
    slot_hot = jnp.arange(devices * capacity, dtype=jnp.int32)[:, None] == slots[None, :]
    col_buffer = jnp.sum(jnp.where(slot_hot, (marker_column + 1)[None, :], 0), axis=1) - 1
    col_buffer = col_buffer.reshape(size_x, size_y, capacity)
    slot_matrix = slot_hot.astype(jnp.float32)
    payload = jnp.stack([marker_value, marker_height], axis=1)
    marks = payload.shape[2]
    send_buf = jnp.dot(
        slot_matrix,
        payload.reshape(block_rows, 2 * marks),
        precision=lax.Precision.HIGHEST,
        preferred_element_type=jnp.float32,
    )
    send_buf = send_buf.reshape(size_x, size_y, capacity, 2, marks)
    arrived, arrived_cols = (
        lax.all_to_all(
            lax.all_to_all(send_buf, "gx", split_axis=0, concat_axis=0, tiled=True),
            "gy",
            split_axis=1,
            concat_axis=1,
            tiled=True,
        ),
        lax.all_to_all(
            lax.all_to_all(col_buffer, "gx", split_axis=0, concat_axis=0, tiled=True),
            "gy",
            split_axis=1,
            concat_axis=1,
            tiled=True,
        ),
    )
    arrived = arrived.reshape(devices * capacity, 2, marks)
    arrived_cols = arrived_cols.reshape(devices * capacity)
    rows = jnp.where(arrived_cols >= 0, arrived_cols, columns_n).astype(jnp.int32)
    profile = column_profile(arrived[:, 0], arrived[:, 1], num_levels)
    sums = place_rows(rows, profile, columns_n)
    sums = sums.reshape(cells_x, cells_y, 2, num_levels)
    viscosity = jnp.exp((sums[:, :, 0] + background) / (sums[:, :, 1] + 1.0))
    global_x = lax.axis_index("gx") * cells_x + jnp.arange(cells_x)
    global_y = lax.axis_index("gy") * cells_y + jnp.arange(cells_y)
    mask_x = (global_x < cells_x * size_x - 1).astype(jnp.float32)
    mask_y = (global_y < cells_y * size_y - 1).astype(jnp.float32)
    mask_z = (jnp.arange(num_levels) < num_levels - 1).astype(jnp.float32)
    ones_grid = jnp.ones((cells_x, cells_y, num_levels), jnp.float32)
    masks = jnp.stack(
        [
            ones_grid * mask_x[:, None, None],
            ones_grid * mask_y[None, :, None],
            ones_grid * mask_z[None, None, :],
        ]
    )
    vel = velocity
    moment = jnp.zeros_like(velocity)
    visc_pad = rims(viscosity[None])[0]
    press = pressure
    for sweep_idx in range(ITERS):
        press, stress, sig_zz = stresses(rims(vel), visc_pad, press)
        residual = residuals(rims(stress), sig_zz, buoyancy)
        vel, moment = advance(vel, moment, residual, visc_pad, masks)
    return (vel, press, viscosity)


def solution(mesh):
    return jax.shard_map(
        shards,
        mesh=mesh,
        in_specs=(
            P(None, "gx", "gy", None),
            P("gx", "gy", None),
            P("gx", "gy", None),
            P("gx", "gy", None),
            P(("gx", "gy"), None),
            P(("gx", "gy"), None),
            P(("gx", "gy"), None),
            P(("gx", "gy")),
            P(("gx", "gy")),
        ),
        out_specs=(P(None, "gx", "gy", None), P("gx", "gy", None), P("gx", "gy", None)),
        check_vma=False,
    )
```

profile of v0, /device:TPU:1, one launch (start us, length us, event | category | flops | bytes accessed | tf_op | source)
XLA Modules:
  0.0 229.5 jit_solution(1652927440290417424)
XLA Ops:
  5.2 4.3 %all-to-all-start = ((s32[4,1,128]{2,1,0:T(1,128)}), s32[4,1,128]{2,1,0:T(1,128)S(1)}, u32[]{:S(2)}, u32[]{:S(2)}) async-start(s32[4,1,128]{2,1,0:T(1,128)} %reshape.171), calls=%async_computation | async-start | bytes 4096 | tf_op jit(solution)/shard_map/all_to_all | solution.py:196
  13.3 3.5 %all-to-all-start.2 = ((f32[4,8,16,2,256]{4,2,3,1,0:T(8,128)}), f32[4,8,16,2,256]{4,2,3,1,0:T(8,128)S(1)}, u32[]{:S(2)}, u32[]{:S(2)}) async-start(f32[4,8,16,2,256]{4,2,3,1,0:T(8,128)} %fusion.1), calls=%async_computation.2 | async-start | bytes 2097152 | tf_op jit(solution)/shard_map/all_to_all | solution.py:189
  18.7 11.7 %all-to-all-done.2 = f32[4,8,16,2,256]{4,2,3,1,0:T(8,128)S(1)} async-done(((f32[4,8,16,2,256]{4,2,3,1,0:T(8,128)}), f32[4,8,16,2,256]{4,2,3,1,0:T(8,128)S(1)}, u32[]{:S(2)}, u32[]{:S(2)}) %all-to-all-start.2) | async-done | bytes 1048608 | tf_op jit(solution)/shard_map/all_to_all | solution.py:189
  30.4 6.0 %all-to-all-start.1 = ((s32[4,8,16]{2,0,1:T(4,128)}), s32[4,8,16]{2,0,1:T(4,128)S(1)}, u32[]{:S(2)}, u32[]{:S(2)}) async-start(s32[4,8,16]{2,0,1:T(4,128)} %copy.41), calls=%async_computation.1 | async-start | bytes 32768 | tf_op jit(solution)/shard_map/all_to_all | solution.py:195
  37.4 4.4 %all-to-all-done.1 = s32[4,8,16]{2,0,1:T(4,128)S(1)} async-done(((s32[4,8,16]{2,0,1:T(4,128)}), s32[4,8,16]{2,0,1:T(4,128)S(1)}, u32[]{:S(2)}, u32[]{:S(2)}) %all-to-all-start.1) | async-done | bytes 2080 | tf_op jit(solution)/shard_map/all_to_all | solution.py:195
  41.8 3.6 %all-to-all-start.3 = ((f32[4,8,16,2,256]{4,2,3,0,1:T(8,128)}), f32[4,8,16,2,256]{4,2,3,0,1:T(8,128)S(1)}, u32[]{:S(2)}, u32[]{:S(2)}) async-start(f32[4,8,16,2,256]{4,2,3,0,1:T(8,128)} %copy.45), calls=%async_computation.3 | async-start | bytes 2097152 | tf_op jit(solution)/shard_map/all_to_all | solution.py:188
  45.4 4.2 %collective-permute-start.4 = (f32[3,1,8,128]{3,2,1,0:T(8,128)S(1)}, f32[3,1,8,128]{3,2,1,0:T(8,128)S(1)}, u32[]{:S(2)}, u32[]{:S(2)}) collective-permute-start(f32[3,1,8,128]{3,2,1,0:T(8,128)S(1)} %get-tuple-element.49), channel_id=1, source_target_pairs={{0,8},{8,16},{16,24},{1,9},{9,17},{17,25},{2,10},{10,18},{18,26},{... | collective-permute-start | bytes 36872 | tf_op jit(solution)/shard_map/ppermute | solution.py:19
  49.6 1.9 collective-permute-start.5
  51.7 3.2 %collective-permute-done.5 = f32[3,1,8,128]{3,2,1,0:T(8,128)S(1)} collective-permute-done((f32[3,1,8,128]{3,2,1,0:T(8,128)S(1)}, f32[3,1,8,128]{3,2,1,0:T(8,128)S(1)}, u32[]{:S(2)}, u32[]{:S(2)}) %collective-permute-start.5) | collective-permute-done | bytes 12320 | tf_op jit(solution)/shard_map/ppermute | solution.py:20
  54.9 3.5 %collective-permute-start.6 = (f32[3,10,1,128]{3,2,1,0:T(1,128)S(1)}, f32[3,10,1,128]{3,2,1,0:T(1,128)S(1)}, u32[]{:S(2)}, u32[]{:S(2)}) collective-permute-start(f32[3,10,1,128]{3,2,1,0:T(1,128)S(1)} %get-tuple-element.44), channel_id=1, source_target_pairs={{0,1},{1,2},{2,3},{3,4},{4,5},{5,6},{6,7},{8,9},{9,10},{10,11},{11... | collective-permute-start | bytes 46088 | tf_op jit(solution)/shard_map/ppermute | solution.py:19
  59.7 9.4 %all-to-all-done.3 = f32[4,8,16,2,256]{4,2,3,0,1:T(8,128)S(1)} async-done(((f32[4,8,16,2,256]{4,2,3,0,1:T(8,128)}), f32[4,8,16,2,256]{4,2,3,0,1:T(8,128)S(1)}, u32[]{:S(2)}, u32[]{:S(2)}) %all-to-all-start.3) | async-done | bytes 1048608 | tf_op jit(solution)/shard_map/all_to_all | solution.py:188
  69.4 91.5 %multiply_reduce_fusion = (f32[512,128]{1,0:T(8,128)S(1)}, f32[512,128]{1,0:T(8,128)S(1)}) fusion(f32[512,256]{1,0:T(8,128)S(1)} %slice_bitcast_fusion, f32[512,256]{1,0:T(8,128)S(1)} %get-tuple-element.17, s32[512,256]{1,0:T(8,128)S(1)} %broadcast_add_fusion, f32[512,256]{1,0:T(8,128)S(1)} %get-tuple-element.16, s32[512,256]{1,0:T(8,128)S(1)} %get-tuple-element.15), kind=kLoop, calls=%fused_computation | loop fusion | flops 134086656 | bytes 3145728 | tf_op jit(solution)/shard_map/reduce_sum | solution.py:63
  161.8 5.4 %collective-permute-start = (f32[1,1,8,128]{3,2,1,0:T(8,128)S(1)}, f32[1,1,8,128]{3,2,1,0:T(8,128)S(1)}, u32[]{:S(2)}, u32[]{:S(2)}) collective-permute-start(f32[1,1,8,128]{3,2,1,0:T(8,128)S(1)} %get-tuple-element.62), channel_id=1, source_target_pairs={{0,8},{8,16},{16,24},{1,9},{9,17},{17,25},{2,10},{10,18},{18,26},{... | collective-permute-start | bytes 12296 | tf_op jit(solution)/shard_map/ppermute | solution.py:19
  167.2 1.9 collective-permute-start.1
  169.2 2.9 %collective-permute-done.1 = f32[1,1,8,128]{3,2,1,0:T(8,128)S(1)} collective-permute-done((f32[1,1,8,128]{3,2,1,0:T(8,128)S(1)}, f32[1,1,8,128]{3,2,1,0:T(8,128)S(1)}, u32[]{:S(2)}, u32[]{:S(2)}) %collective-permute-start.1) | collective-permute-done | bytes 4128 | tf_op jit(solution)/shard_map/ppermute | solution.py:20
  172.2 2.7 %collective-permute-start.2 = (f32[1,10,1,128]{3,2,1,0:T(1,128)S(1)}, f32[1,10,1,128]{3,2,1,0:T(1,128)S(1)}, u32[]{:S(2)}, u32[]{:S(2)}) collective-permute-start(f32[1,10,1,128]{3,2,1,0:T(1,128)S(1)} %get-tuple-element.60), channel_id=1, source_target_pairs={{0,1},{1,2},{2,3},{3,4},{4,5},{5,6},{6,7},{8,9},{9,10},{10,11},{11... | collective-permute-start | bytes 15368 | tf_op jit(solution)/shard_map/ppermute | solution.py:19
  176.4 2.9 %collective-permute-done.3 = f32[1,10,1,128]{3,2,1,0:T(1,128)S(1)} collective-permute-done((f32[1,10,1,128]{3,2,1,0:T(1,128)S(1)}, f32[1,10,1,128]{3,2,1,0:T(1,128)S(1)}, u32[]{:S(2)}, u32[]{:S(2)}) %collective-permute-start.3) | collective-permute-done | bytes 5152 | tf_op jit(solution)/shard_map/ppermute | solution.py:20
  179.8 3.4 %collective-permute-start.8 = (f32[5,1,8,128]{3,2,1,0:T(8,128)S(1)}, f32[5,1,8,128]{3,2,1,0:T(8,128)S(1)}, u32[]{:S(2)}, u32[]{:S(2)}) collective-permute-start(f32[5,1,8,128]{3,2,1,0:T(8,128)S(1)} %get-tuple-element.40), channel_id=1, source_target_pairs={{0,8},{8,16},{16,24},{1,9},{9,17},{17,25},{2,10},{10,18},{18,26},{... | collective-permute-start | bytes 61448 | tf_op jit(solution)/shard_map/ppermute | solution.py:19
  183.2 1.9 collective-permute-start.9
  185.1 3.1 %collective-permute-done.9 = f32[5,1,8,128]{3,2,1,0:T(8,128)S(1)} collective-permute-done((f32[5,1,8,128]{3,2,1,0:T(8,128)S(1)}, f32[5,1,8,128]{3,2,1,0:T(8,128)S(1)}, u32[]{:S(2)}, u32[]{:S(2)}) %collective-permute-start.9) | collective-permute-done | bytes 20512 | tf_op jit(solution)/shard_map/ppermute | solution.py:20
  188.3 2.5 %collective-permute-start.10 = (f32[5,10,1,128]{3,2,1,0:T(1,128)S(1)}, f32[5,10,1,128]{3,2,1,0:T(1,128)S(1)}, u32[]{:S(2)}, u32[]{:S(2)}) collective-permute-start(f32[5,10,1,128]{3,2,1,0:T(1,128)S(1)} %get-tuple-element.36), channel_id=1, source_target_pairs={{0,1},{1,2},{2,3},{3,4},{4,5},{5,6},{6,7},{8,9},{9,10},{10,11},{11... | collective-permute-start | bytes 76808 | tf_op jit(solution)/shard_map/ppermute | solution.py:19
  192.3 3.2 %collective-permute-done.11 = f32[5,10,1,128]{3,2,1,0:T(1,128)S(1)} collective-permute-done((f32[5,10,1,128]{3,2,1,0:T(1,128)S(1)}, f32[5,10,1,128]{3,2,1,0:T(1,128)S(1)}, u32[]{:S(2)}, u32[]{:S(2)}) %collective-permute-start.11) | collective-permute-done | bytes 25632 | tf_op jit(solution)/shard_map/ppermute | solution.py:20
  195.9 3.4 %collective-permute-start.12 = (f32[3,1,8,128]{3,2,1,0:T(8,128)S(1)}, f32[3,1,8,128]{3,2,1,0:T(8,128)S(1)}, u32[]{:S(2)}, u32[]{:S(2)}) collective-permute-start(f32[3,1,8,128]{3,2,1,0:T(8,128)S(1)} %get-tuple-element.46), channel_id=1, source_target_pairs={{0,8},{8,16},{16,24},{1,9},{9,17},{17,25},{2,10},{10,18},{18,26},{... | collective-permute-start | bytes 36872 | tf_op jit(solution)/shard_map/ppermute | solution.py:19
  199.3 1.9 collective-permute-start.13
  201.2 3.1 %collective-permute-done.13 = f32[3,1,8,128]{3,2,1,0:T(8,128)S(1)} collective-permute-done((f32[3,1,8,128]{3,2,1,0:T(8,128)S(1)}, f32[3,1,8,128]{3,2,1,0:T(8,128)S(1)}, u32[]{:S(2)}, u32[]{:S(2)}) %collective-permute-start.13) | collective-permute-done | bytes 12320 | tf_op jit(solution)/shard_map/ppermute | solution.py:20
  204.3 2.5 %collective-permute-start.14 = (f32[3,10,1,128]{3,2,1,0:T(1,128)S(1)}, f32[3,10,1,128]{3,2,1,0:T(1,128)S(1)}, u32[]{:S(2)}, u32[]{:S(2)}) collective-permute-start(f32[3,10,1,128]{3,2,1,0:T(1,128)S(1)} %get-tuple-element.42), channel_id=1, source_target_pairs={{0,1},{1,2},{2,3},{3,4},{4,5},{5,6},{6,7},{8,9},{9,10},{10,11},{11... | collective-permute-start | bytes 46088 | tf_op jit(solution)/shard_map/ppermute | solution.py:19
  208.2 3.2 %collective-permute-done.15 = f32[3,10,1,128]{3,2,1,0:T(1,128)S(1)} collective-permute-done((f32[3,10,1,128]{3,2,1,0:T(1,128)S(1)}, f32[3,10,1,128]{3,2,1,0:T(1,128)S(1)}, u32[]{:S(2)}, u32[]{:S(2)}) %collective-permute-start.15) | collective-permute-done | bytes 15392 | tf_op jit(solution)/shard_map/ppermute | solution.py:20
  211.8 3.4 %collective-permute-start.16 = (f32[5,1,8,128]{3,2,1,0:T(8,128)S(1)}, f32[5,1,8,128]{3,2,1,0:T(8,128)S(1)}, u32[]{:S(2)}, u32[]{:S(2)}) collective-permute-start(f32[5,1,8,128]{3,2,1,0:T(8,128)S(1)} %get-tuple-element.38), channel_id=1, source_target_pairs={{0,8},{8,16},{16,24},{1,9},{9,17},{17,25},{2,10},{10,18},{18,26},{... | collective-permute-start | bytes 61448 | tf_op jit(solution)/shard_map/ppermute | solution.py:19
  215.2 1.9 collective-permute-start.17
  217.1 3.2 %collective-permute-done.17 = f32[5,1,8,128]{3,2,1,0:T(8,128)S(1)} collective-permute-done((f32[5,1,8,128]{3,2,1,0:T(8,128)S(1)}, f32[5,1,8,128]{3,2,1,0:T(8,128)S(1)}, u32[]{:S(2)}, u32[]{:S(2)}) %collective-permute-start.17) | collective-permute-done | bytes 20512 | tf_op jit(solution)/shard_map/ppermute | solution.py:20
  220.3 3.7 %collective-permute-start.18 = (f32[5,10,1,128]{3,2,1,0:T(1,128)S(1)}, f32[5,10,1,128]{3,2,1,0:T(1,128)S(1)}, u32[]{:S(2)}, u32[]{:S(2)}) collective-permute-start(f32[5,10,1,128]{3,2,1,0:T(1,128)S(1)} %get-tuple-element.34), channel_id=1, source_target_pairs={{0,1},{1,2},{2,3},{3,4},{4,5},{5,6},{6,7},{8,9},{9,10},{10,11},{11... | collective-permute-start | bytes 76808 | tf_op jit(solution)/shard_map/ppermute | solution.py:19
  225.5 3.1 %collective-permute-done.19 = f32[5,10,1,128]{3,2,1,0:T(1,128)S(1)} collective-permute-done((f32[5,10,1,128]{3,2,1,0:T(1,128)S(1)}, f32[5,10,1,128]{3,2,1,0:T(1,128)S(1)}, u32[]{:S(2)}, u32[]{:S(2)}) %collective-permute-start.19) | collective-permute-done | bytes 25632 | tf_op jit(solution)/shard_map/ppermute | solution.py:20
  (123 shorter events, 21.2 us)
Async XLA Ops:
  5.2 8.1 %all-to-all-start = ((s32[4,1,128]{2,1,0:T(1,128)}), s32[4,1,128]{2,1,0:T(1,128)S(1)}, u32[]{:S(2)}, u32[]{:S(2)}) async-start(s32[4,1,128]{2,1,0:T(1,128)} %reshape.171), calls=%async_computation | async-start | bytes 4096 | tf_op jit(solution)/shard_map/all_to_all | solution.py:196
  13.3 17.1 %all-to-all-start.2 = ((f32[4,8,16,2,256]{4,2,3,1,0:T(8,128)}), f32[4,8,16,2,256]{4,2,3,1,0:T(8,128)S(1)}, u32[]{:S(2)}, u32[]{:S(2)}) async-start(f32[4,8,16,2,256]{4,2,3,1,0:T(8,128)} %fusion.1), calls=%async_computation.2 | async-start | bytes 2097152 | tf_op jit(solution)/shard_map/all_to_all | solution.py:189
  30.4 11.4 %all-to-all-start.1 = ((s32[4,8,16]{2,0,1:T(4,128)}), s32[4,8,16]{2,0,1:T(4,128)S(1)}, u32[]{:S(2)}, u32[]{:S(2)}) async-start(s32[4,8,16]{2,0,1:T(4,128)} %copy.41), calls=%async_computation.1 | async-start | bytes 32768 | tf_op jit(solution)/shard_map/all_to_all | solution.py:195
  37.4 7.9 %copy-start = (f32[3,8,8,128]{3,2,1,0:T(8,128)S(1)}, f32[3,8,8,128]{3,2,1,0:T(8,128)}, u32[]{:S(2)}) copy-start(f32[3,8,8,128]{3,2,1,0:T(8,128)} %param.9) | copy-start | bytes 294916
  41.8 27.3 %all-to-all-start.3 = ((f32[4,8,16,2,256]{4,2,3,0,1:T(8,128)}), f32[4,8,16,2,256]{4,2,3,0,1:T(8,128)S(1)}, u32[]{:S(2)}, u32[]{:S(2)}) async-start(f32[4,8,16,2,256]{4,2,3,0,1:T(8,128)} %copy.45), calls=%async_computation.3 | async-start | bytes 2097152 | tf_op jit(solution)/shard_map/all_to_all | solution.py:188
  45.4 6.3 %collective-permute-start.4 = (f32[3,1,8,128]{3,2,1,0:T(8,128)S(1)}, f32[3,1,8,128]{3,2,1,0:T(8,128)S(1)}, u32[]{:S(2)}, u32[]{:S(2)}) collective-permute-start(f32[3,1,8,128]{3,2,1,0:T(8,128)S(1)} %get-tuple-element.49), channel_id=1, source_target_pairs={{0,8},{8,16},{16,24},{1,9},{9,17},{17,25},{2,10},{10,18},{18,26},{... | collective-permute-start | bytes 36872 | tf_op jit(solution)/shard_map/ppermute | solution.py:19
  49.6 5.3 %collective-permute-start.5 = (f32[3,1,8,128]{3,2,1,0:T(8,128)S(1)}, f32[3,1,8,128]{3,2,1,0:T(8,128)S(1)}, u32[]{:S(2)}, u32[]{:S(2)}) collective-permute-start(f32[3,1,8,128]{3,2,1,0:T(8,128)S(1)} %get-tuple-element.48), channel_id=1, source_target_pairs={{8,0},{16,8},{24,16},{9,1},{17,9},{25,17},{10,2},{18,10},{26,18},{... | collective-permute-start | bytes 36872 | tf_op jit(solution)/shard_map/ppermute | solution.py:20
  54.9 114.3 %collective-permute-start.6 = (f32[3,10,1,128]{3,2,1,0:T(1,128)S(1)}, f32[3,10,1,128]{3,2,1,0:T(1,128)S(1)}, u32[]{:S(2)}, u32[]{:S(2)}) collective-permute-start(f32[3,10,1,128]{3,2,1,0:T(1,128)S(1)} %get-tuple-element.44), channel_id=1, source_target_pairs={{0,1},{1,2},{2,3},{3,4},{4,5},{5,6},{6,7},{8,9},{9,10},{10,11},{11... | collective-permute-start | bytes 46088 | tf_op jit(solution)/shard_map/ppermute | solution.py:19
  58.4 110.7 %collective-permute-start.7 = (f32[3,10,1,128]{3,2,1,0:T(1,128)S(1)}, f32[3,10,1,128]{3,2,1,0:T(1,128)S(1)}, u32[]{:S(2)}, u32[]{:S(2)}) collective-permute-start(f32[3,10,1,128]{3,2,1,0:T(1,128)S(1)} %get-tuple-element.45), channel_id=1, source_target_pairs={{1,0},{2,1},{3,2},{4,3},{5,4},{6,5},{7,6},{9,8},{10,9},{11,10},{12... | collective-permute-start | bytes 46088 | tf_op jit(solution)/shard_map/ppermute | solution.py:20
  161.0 0.8 copy-start.4
  161.2 18.1 %copy-start.5 = (f32[8,8,128]{2,1,0:T(8,128)S(1)}, f32[8,8,128]{2,1,0:T(8,128)}, u32[]{:S(2)}) copy-start(f32[8,8,128]{2,1,0:T(8,128)} %param.10) | copy-start | bytes 98308
  161.8 17.7 %copy-start.1 = (f32[8,8,128]{2,1,0:T(8,128)}, f32[8,8,128]{2,1,0:T(8,128)S(1)}, u32[]{:S(2)}) copy-start(f32[8,8,128]{2,1,0:T(8,128)S(1)} %fusion.74) | copy-start | bytes 98308
  161.8 7.4 %collective-permute-start = (f32[1,1,8,128]{3,2,1,0:T(8,128)S(1)}, f32[1,1,8,128]{3,2,1,0:T(8,128)S(1)}, u32[]{:S(2)}, u32[]{:S(2)}) collective-permute-start(f32[1,1,8,128]{3,2,1,0:T(8,128)S(1)} %get-tuple-element.62), channel_id=1, source_target_pairs={{0,8},{8,16},{16,24},{1,9},{9,17},{17,25},{2,10},{10,18},{18,26},{... | collective-permute-start | bytes 12296 | tf_op jit(solution)/shard_map/ppermute | solution.py:19
  167.2 4.9 %collective-permute-start.1 = (f32[1,1,8,128]{3,2,1,0:T(8,128)S(1)}, f32[1,1,8,128]{3,2,1,0:T(8,128)S(1)}, u32[]{:S(2)}, u32[]{:S(2)}) collective-permute-start(f32[1,1,8,128]{3,2,1,0:T(8,128)S(1)} %get-tuple-element.63), channel_id=1, source_target_pairs={{8,0},{16,8},{24,16},{9,1},{17,9},{25,17},{10,2},{18,10},{26,18},{... | collective-permute-start | bytes 12296 | tf_op jit(solution)/shard_map/ppermute | solution.py:20
  172.2 4.2 %collective-permute-start.2 = (f32[1,10,1,128]{3,2,1,0:T(1,128)S(1)}, f32[1,10,1,128]{3,2,1,0:T(1,128)S(1)}, u32[]{:S(2)}, u32[]{:S(2)}) collective-permute-start(f32[1,10,1,128]{3,2,1,0:T(1,128)S(1)} %get-tuple-element.60), channel_id=1, source_target_pairs={{0,1},{1,2},{2,3},{3,4},{4,5},{5,6},{6,7},{8,9},{9,10},{10,11},{11... | collective-permute-start | bytes 15368 | tf_op jit(solution)/shard_map/ppermute | solution.py:19
  174.9 4.4 %collective-permute-start.3 = (f32[1,10,1,128]{3,2,1,0:T(1,128)S(1)}, f32[1,10,1,128]{3,2,1,0:T(1,128)S(1)}, u32[]{:S(2)}, u32[]{:S(2)}) collective-permute-start(f32[1,10,1,128]{3,2,1,0:T(1,128)S(1)} %get-tuple-element.61), channel_id=1, source_target_pairs={{1,0},{2,1},{3,2},{4,3},{5,4},{6,5},{7,6},{9,8},{10,9},{11,10},{12... | collective-permute-start | bytes 15368 | tf_op jit(solution)/shard_map/ppermute | solution.py:20
  179.8 15.8 %copy-start.3 = (f32[8,8,128]{2,1,0:T(8,128)S(1)}, f32[8,8,128]{2,1,0:T(8,128)}, u32[]{:S(2)}) copy-start(f32[8,8,128]{2,1,0:T(8,128)} %param.11) | copy-start | bytes 98308
  179.8 5.3 %collective-permute-start.8 = (f32[5,1,8,128]{3,2,1,0:T(8,128)S(1)}, f32[5,1,8,128]{3,2,1,0:T(8,128)S(1)}, u32[]{:S(2)}, u32[]{:S(2)}) collective-permute-start(f32[5,1,8,128]{3,2,1,0:T(8,128)S(1)} %get-tuple-element.40), channel_id=1, source_target_pairs={{0,8},{8,16},{16,24},{1,9},{9,17},{17,25},{2,10},{10,18},{18,26},{... | collective-permute-start | bytes 61448 | tf_op jit(solution)/shard_map/ppermute | solution.py:19
  183.2 5.1 %collective-permute-start.9 = (f32[5,1,8,128]{3,2,1,0:T(8,128)S(1)}, f32[5,1,8,128]{3,2,1,0:T(8,128)S(1)}, u32[]{:S(2)}, u32[]{:S(2)}) collective-permute-start(f32[5,1,8,128]{3,2,1,0:T(8,128)S(1)} %get-tuple-element.41), channel_id=1, source_target_pairs={{8,0},{16,8},{24,16},{9,1},{17,9},{25,17},{10,2},{18,10},{26,18},{... | collective-permute-start | bytes 61448 | tf_op jit(solution)/shard_map/ppermute | solution.py:20
  188.3 3.9 %collective-permute-start.10 = (f32[5,10,1,128]{3,2,1,0:T(1,128)S(1)}, f32[5,10,1,128]{3,2,1,0:T(1,128)S(1)}, u32[]{:S(2)}, u32[]{:S(2)}) collective-permute-start(f32[5,10,1,128]{3,2,1,0:T(1,128)S(1)} %get-tuple-element.36), channel_id=1, source_target_pairs={{0,1},{1,2},{2,3},{3,4},{4,5},{5,6},{6,7},{8,9},{9,10},{10,11},{11... | collective-permute-start | bytes 76808 | tf_op jit(solution)/shard_map/ppermute | solution.py:19
  190.9 4.6 %collective-permute-start.11 = (f32[5,10,1,128]{3,2,1,0:T(1,128)S(1)}, f32[5,10,1,128]{3,2,1,0:T(1,128)S(1)}, u32[]{:S(2)}, u32[]{:S(2)}) collective-permute-start(f32[5,10,1,128]{3,2,1,0:T(1,128)S(1)} %get-tuple-element.37), channel_id=1, source_target_pairs={{1,0},{2,1},{3,2},{4,3},{5,4},{6,5},{7,6},{9,8},{10,9},{11,10},{12... | collective-permute-start | bytes 76808 | tf_op jit(solution)/shard_map/ppermute | solution.py:20
  195.9 5.3 %collective-permute-start.12 = (f32[3,1,8,128]{3,2,1,0:T(8,128)S(1)}, f32[3,1,8,128]{3,2,1,0:T(8,128)S(1)}, u32[]{:S(2)}, u32[]{:S(2)}) collective-permute-start(f32[3,1,8,128]{3,2,1,0:T(8,128)S(1)} %get-tuple-element.46), channel_id=1, source_target_pairs={{0,8},{8,16},{16,24},{1,9},{9,17},{17,25},{2,10},{10,18},{18,26},{... | collective-permute-start | bytes 36872 | tf_op jit(solution)/shard_map/ppermute | solution.py:19
  199.3 5.0 %collective-permute-start.13 = (f32[3,1,8,128]{3,2,1,0:T(8,128)S(1)}, f32[3,1,8,128]{3,2,1,0:T(8,128)S(1)}, u32[]{:S(2)}, u32[]{:S(2)}) collective-permute-start(f32[3,1,8,128]{3,2,1,0:T(8,128)S(1)} %get-tuple-element.47), channel_id=1, source_target_pairs={{8,0},{16,8},{24,16},{9,1},{17,9},{25,17},{10,2},{18,10},{26,18},{... | collective-permute-start | bytes 36872 | tf_op jit(solution)/shard_map/ppermute | solution.py:20
  204.3 3.8 %collective-permute-start.14 = (f32[3,10,1,128]{3,2,1,0:T(1,128)S(1)}, f32[3,10,1,128]{3,2,1,0:T(1,128)S(1)}, u32[]{:S(2)}, u32[]{:S(2)}) collective-permute-start(f32[3,10,1,128]{3,2,1,0:T(1,128)S(1)} %get-tuple-element.42), channel_id=1, source_target_pairs={{0,1},{1,2},{2,3},{3,4},{4,5},{5,6},{6,7},{8,9},{9,10},{10,11},{11... | collective-permute-start | bytes 46088 | tf_op jit(solution)/shard_map/ppermute | solution.py:19
  206.8 4.5 %collective-permute-start.15 = (f32[3,10,1,128]{3,2,1,0:T(1,128)S(1)}, f32[3,10,1,128]{3,2,1,0:T(1,128)S(1)}, u32[]{:S(2)}, u32[]{:S(2)}) collective-permute-start(f32[3,10,1,128]{3,2,1,0:T(1,128)S(1)} %get-tuple-element.43), channel_id=1, source_target_pairs={{1,0},{2,1},{3,2},{4,3},{5,4},{6,5},{7,6},{9,8},{10,9},{11,10},{12... | collective-permute-start | bytes 46088 | tf_op jit(solution)/shard_map/ppermute | solution.py:20
  211.7 17.0 %copy-start.2 = (f32[8,8,128]{2,1,0:T(8,128)}, f32[8,8,128]{2,1,0:T(8,128)S(1)}, u32[]{:S(2)}) copy-start(f32[8,8,128]{2,1,0:T(8,128)S(1)} %get-tuple-element.6) | copy-start | bytes 98308
  211.8 5.3 %collective-permute-start.16 = (f32[5,1,8,128]{3,2,1,0:T(8,128)S(1)}, f32[5,1,8,128]{3,2,1,0:T(8,128)S(1)}, u32[]{:S(2)}, u32[]{:S(2)}) collective-permute-start(f32[5,1,8,128]{3,2,1,0:T(8,128)S(1)} %get-tuple-element.38), channel_id=1, source_target_pairs={{0,8},{8,16},{16,24},{1,9},{9,17},{17,25},{2,10},{10,18},{18,26},{... | collective-permute-start | bytes 61448 | tf_op jit(solution)/shard_map/ppermute | solution.py:19
  215.2 5.1 %collective-permute-start.17 = (f32[5,1,8,128]{3,2,1,0:T(8,128)S(1)}, f32[5,1,8,128]{3,2,1,0:T(8,128)S(1)}, u32[]{:S(2)}, u32[]{:S(2)}) collective-permute-start(f32[5,1,8,128]{3,2,1,0:T(8,128)S(1)} %get-tuple-element.39), channel_id=1, source_target_pairs={{8,0},{16,8},{24,16},{9,1},{17,9},{25,17},{10,2},{18,10},{26,18},{... | collective-permute-start | bytes 61448 | tf_op jit(solution)/shard_map/ppermute | solution.py:20
  220.3 5.1 %collective-permute-start.18 = (f32[5,10,1,128]{3,2,1,0:T(1,128)S(1)}, f32[5,10,1,128]{3,2,1,0:T(1,128)S(1)}, u32[]{:S(2)}, u32[]{:S(2)}) collective-permute-start(f32[5,10,1,128]{3,2,1,0:T(1,128)S(1)} %get-tuple-element.34), channel_id=1, source_target_pairs={{0,1},{1,2},{2,3},{3,4},{4,5},{5,6},{6,7},{8,9},{9,10},{10,11},{11... | collective-permute-start | bytes 76808 | tf_op jit(solution)/shard_map/ppermute | solution.py:19
  224.0 4.6 %collective-permute-start.19 = (f32[5,10,1,128]{3,2,1,0:T(1,128)S(1)}, f32[5,10,1,128]{3,2,1,0:T(1,128)S(1)}, u32[]{:S(2)}, u32[]{:S(2)}) collective-permute-start(f32[5,10,1,128]{3,2,1,0:T(1,128)S(1)} %get-tuple-element.35), channel_id=1, source_target_pairs={{1,0},{2,1},{3,2},{4,3},{5,4},{6,5},{7,6},{9,8},{10,9},{11,10},{12... | collective-permute-start | bytes 76808 | tf_op jit(solution)/shard_map/ppermute | solution.py:20
where the time goes:
time: 231 us; the launch traced here: 230 us
  other arithmetic  97.2 us (42%)
  starting transfers between devices  68 us (29%)
  waiting for transfers between devices  53.3 us (23%)
  local copies, waits for them, and re-layouts  6.92 us (3%)
    reduce_sum x1, other arithmetic, column_profile(): value_sum = jnp.sum(weight * values[..., None], axis=1)  91.5 us
    ppermute x10, starting transfers between devices, extended(): before = lax.ppermute(last, axis, up)  34.7 us
    ppermute x10, waiting for transfers between devices, extended(): after = lax.ppermute(first, axis, down)  27.8 us
    ppermute x10, starting transfers between devices, extended(): after = lax.ppermute(first, axis, down)  16.1 us
    all_to_all x1, waiting for transfers between devices, shards(): lax.all_to_all(send_buf, 'gx', split_axis=0, concat_axis=0, tiled=True)  11.7 us
    all_to_all x1, waiting for transfers between devices, shards(): lax.all_to_all(lax.all_to_all(send_buf, 'gx', split_axis=0, concat_axis=0...  9.35 us
    all_to_all x1, starting transfers between devices, shards(): lax.all_to_all(lax.all_to_all(col_buffer, 'gx', split_axis=0, concat_axis...  5.98 us
  transfers between devices with their start and end apart: 24, of which 12 were waited for; matrix products, arithmetic and copies ran while one was open for 43% of the time, Pallas kernels for 0%

commit v1 on v0

--- a/solution.py
+++ b/solution.py
@@ -7,6 +7,29 @@
 PRESS_STEP = 0.5
 VEL_STEP = 0.05
 DAMPING = 0.8
+
+
+def cut_along(x, dim, peers):
+    dims = x.shape
+    parts = x.reshape(*dims[:dim], peers, dims[dim] // peers, *dims[dim + 1 :])
+    return jnp.moveaxis(parts, dim, 0)
+
+
+def laid_out(tiles, dim):
+    lengths = list(tiles.shape[1:])
+    lengths[dim] *= tiles.shape[0]
+    return jnp.moveaxis(tiles, 0, dim).reshape(lengths)
+
+
+def rotated_exchange(x, axis, split_dim, concat_dim):
+    peers, index = (lax.axis_size(axis), lax.axis_index(axis))
+    blocks = cut_along(x, split_dim, peers)
+    done = [blocks[index]]
+    for hop in range(1, peers):
+        sent = blocks[(index + hop) % peers]
+        done.append(lax.ppermute(sent, axis, [(i, (i + hop) % peers) for i in range(peers)]))
+    blocks = jnp.stack(done)[(index - jnp.arange(peers)) % peers]
+    return laid_out(blocks, concat_dim)
 
 
 def extended(x, sides, width):
@@ -186,11 +209,7 @@
     send_buf = send_buf.reshape(size_x, size_y, capacity, 2, marks)
     arrived, arrived_cols = (
         lax.all_to_all(
-            lax.all_to_all(send_buf, "gx", split_axis=0, concat_axis=0, tiled=True),
-            "gy",
-            split_axis=1,
-            concat_axis=1,
-            tiled=True,
+            rotated_exchange(send_buf, "gx", 0, 0), "gy", split_axis=1, concat_axis=1, tiled=True
         ),
         lax.all_to_all(
             lax.all_to_all(col_buffer, "gx", split_axis=0, concat_axis=0, tiled=True),

time: 231 us -> 224 us (0.970)
  waiting for transfers between devices: 53.3 us -> 45.1 us
  starting transfers between devices: 68 us -> 70.6 us
    all_to_all x2 -> x1, waiting for transfers between devices: 21.1 us -> 7.91 us  [shards(): lax.all_to_all(rotated_exchange(send_buf, 'gx', 0, 0), 'gy', split_axis=1...]
    all_to_all x1, waiting for transfers between devices: 0.01 us -> 5.72 us  [shards(): lax.all_to_all(col_buffer, 'gx', split_axis=0, concat_axis=0, tiled=True)]
    all_to_all x2 -> x1, starting transfers between devices: 7.06 us -> 3.56 us  [shards(): lax.all_to_all(rotated_exchange(send_buf, 'gx', 0, 0), 'gy', split_axis=1...]
    ppermute x0 -> x3, starting transfers between devices: none -> 3.15 us  [rotated_exchange(): lax.ppermute(sent, axis, [(i, (i + hop) % peers) for i in range(peers)])]
    ppermute x10, starting transfers between devices: 34.7 us -> 37 us  [extended(): before = lax.ppermute(last, axis, up)]
  transfers between devices with their start and end apart: 24 -> 26, of which waited for: 12 -> 12; matrix products, arithmetic and copies ran while one was open for 43% -> 44% of each run, Pallas kernels for 0% -> 0%
where the time goes in v1:
time: 224 us; the launch traced here: 223 us
  other arithmetic  96 us (43%)
  starting transfers between devices  70.6 us (32%)
  waiting for transfers between devices  45.1 us (20%)
  local copies, waits for them, and re-layouts  7.65 us (3%)
    reduce_sum x1, other arithmetic, column_profile(): value_sum = jnp.sum(weight * values[..., None], axis=1)  91.5 us
    ppermute x10, starting transfers between devices, extended(): before = lax.ppermute(last, axis, up)  37 us
    ppermute x10, waiting for transfers between devices, extended(): after = lax.ppermute(first, axis, down)  27.8 us
    ppermute x10, starting transfers between devices, extended(): after = lax.ppermute(first, axis, down)  16.1 us
    all_to_all x1, waiting for transfers between devices, shards(): lax.all_to_all(rotated_exchange(send_buf, 'gx', 0, 0), 'gy', split_axis=1...  7.91 us
    all_to_all x1, starting transfers between devices, shards(): lax.all_to_all(lax.all_to_all(col_buffer, 'gx', split_axis=0, concat_axis...  6.31 us
    all_to_all x1, waiting for transfers between devices, shards(): lax.all_to_all(col_buffer, 'gx', split_axis=0, concat_axis=0, tiled=True)  5.72 us
    all_to_all x1, starting transfers between devices, shards(): lax.all_to_all(col_buffer, 'gx', split_axis=0, concat_axis=0, tiled=True)  4.58 us
  transfers between devices with their start and end apart: 26, of which 12 were waited for; matrix products, arithmetic and copies ran while one was open for 44% of the time, Pallas kernels for 0%

profile of v1, /device:TPU:1, one launch (start us, length us, event | category | flops | bytes accessed | tf_op | source)
XLA Modules:
  0.0 222.6 jit_solution(9162652303530708692)
XLA Ops:
  6.0 2.7 %collective-permute-start = (f32[1,8,16,2,256]{4,2,3,1,0:T(8,128)S(1)}, f32[1,8,16,2,256]{4,2,3,1,0:T(8,128)S(1)}, u32[]{:S(2)}, u32[]{:S(2)}) collective-permute-start(f32[1,8,16,2,256]{4,2,3,1,0:T(8,128)S(1)} %get-tuple-element.21), channel_id=1, source_target_pairs={{0,8},{8,16},{16,24},{24,0},{1,9},{9,17},{17,25},{25,1},{2,10},{10... | collective-permute-start | bytes 786440 | tf_op jit(solution)/shard_map/ppermute | solution.py:30
  10.0 4.6 %all-to-all-start = ((s32[4,1,128]{2,1,0:T(1,128)}), s32[4,1,128]{2,1,0:T(1,128)S(1)}, u32[]{:S(2)}, u32[]{:S(2)}) async-start(s32[4,1,128]{2,1,0:T(1,128)} %reshape.244), calls=%async_computation | async-start | bytes 4096 | tf_op jit(solution)/shard_map/all_to_all | solution.py:215
  14.6 5.7 %all-to-all-done = s32[4,1,128]{2,1,0:T(1,128)S(1)} async-done(((s32[4,1,128]{2,1,0:T(1,128)}), s32[4,1,128]{2,1,0:T(1,128)S(1)}, u32[]{:S(2)}, u32[]{:S(2)}) %all-to-all-start) | async-done | bytes 2080 | tf_op jit(solution)/shard_map/all_to_all | solution.py:215
  22.2 6.3 %all-to-all-start.1 = ((s32[4,8,16]{2,0,1:T(4,128)}), s32[4,8,16]{2,0,1:T(4,128)S(1)}, u32[]{:S(2)}, u32[]{:S(2)}) async-start(s32[4,8,16]{2,0,1:T(4,128)} %copy.41), calls=%async_computation.1 | async-start | bytes 32768 | tf_op jit(solution)/shard_map/all_to_all | solution.py:214
  30.3 3.6 %all-to-all-done.1 = s32[4,8,16]{2,0,1:T(4,128)S(1)} async-done(((s32[4,8,16]{2,0,1:T(4,128)}), s32[4,8,16]{2,0,1:T(4,128)S(1)}, u32[]{:S(2)}, u32[]{:S(2)}) %all-to-all-start.1) | async-done | bytes 2080 | tf_op jit(solution)/shard_map/all_to_all | solution.py:214
  33.9 3.6 %all-to-all-start.2 = ((f32[4,8,16,2,256]{4,2,3,0,1:T(8,128)}), f32[4,8,16,2,256]{4,2,3,0,1:T(8,128)S(1)}, u32[]{:S(2)}, u32[]{:S(2)}) async-start(f32[4,8,16,2,256]{4,2,3,0,1:T(8,128)} %copy.45), calls=%async_computation.2 | async-start | bytes 2097152 | tf_op jit(solution)/shard_map/all_to_all | solution.py:211
  37.5 5.1 %collective-permute-start.7 = (f32[3,1,8,128]{3,2,1,0:T(8,128)S(1)}, f32[3,1,8,128]{3,2,1,0:T(8,128)S(1)}, u32[]{:S(2)}, u32[]{:S(2)}) collective-permute-start(f32[3,1,8,128]{3,2,1,0:T(8,128)S(1)} %get-tuple-element.53), channel_id=1, source_target_pairs={{0,8},{8,16},{16,24},{1,9},{9,17},{17,25},{2,10},{10,18},{18,26},{... | collective-permute-start | bytes 36872 | tf_op jit(solution)/shard_map/ppermute | solution.py:42
  42.6 1.9 collective-permute-start.8
  44.7 3.2 %collective-permute-done.8 = f32[3,1,8,128]{3,2,1,0:T(8,128)S(1)} collective-permute-done((f32[3,1,8,128]{3,2,1,0:T(8,128)S(1)}, f32[3,1,8,128]{3,2,1,0:T(8,128)S(1)}, u32[]{:S(2)}, u32[]{:S(2)}) %collective-permute-start.8) | collective-permute-done | bytes 12320 | tf_op jit(solution)/shard_map/ppermute | solution.py:43
  49.3 4.2 %collective-permute-start.9 = (f32[3,10,1,128]{3,2,1,0:T(1,128)S(1)}, f32[3,10,1,128]{3,2,1,0:T(1,128)S(1)}, u32[]{:S(2)}, u32[]{:S(2)}) collective-permute-start(f32[3,10,1,128]{3,2,1,0:T(1,128)S(1)} %get-tuple-element.48), channel_id=1, source_target_pairs={{0,1},{1,2},{2,3},{3,4},{4,5},{5,6},{6,7},{8,9},{9,10},{10,11},{11... | collective-permute-start | bytes 46088 | tf_op jit(solution)/shard_map/ppermute | solution.py:42
  53.4 7.9 %all-to-all-done.2 = f32[4,8,16,2,256]{4,2,3,0,1:T(8,128)S(1)} async-done(((f32[4,8,16,2,256]{4,2,3,0,1:T(8,128)}), f32[4,8,16,2,256]{4,2,3,0,1:T(8,128)S(1)}, u32[]{:S(2)}, u32[]{:S(2)}) %all-to-all-start.2) | async-done | bytes 1048608 | tf_op jit(solution)/shard_map/all_to_all | solution.py:211
  61.7 91.5 %multiply_reduce_fusion = (f32[512,128]{1,0:T(8,128)S(1)}, f32[512,128]{1,0:T(8,128)S(1)}) fusion(f32[512,256]{1,0:T(8,128)S(1)} %slice_bitcast_fusion, f32[512,256]{1,0:T(8,128)S(1)} %get-tuple-element.17, s32[512,256]{1,0:T(8,128)S(1)} %broadcast_add_fusion, f32[512,256]{1,0:T(8,128)S(1)} %get-tuple-element.16, s32[512,256]{1,0:T(8,128)S(1)} %get-tuple-element.15), kind=kLoop, calls=%fused_computation.1 | loop fusion | flops 134086656 | bytes 3145728 | tf_op jit(solution)/shard_map/reduce_sum | solution.py:86
  154.1 6.2 %collective-permute-start.3 = (f32[1,1,8,128]{3,2,1,0:T(8,128)S(1)}, f32[1,1,8,128]{3,2,1,0:T(8,128)S(1)}, u32[]{:S(2)}, u32[]{:S(2)}) collective-permute-start(f32[1,1,8,128]{3,2,1,0:T(8,128)S(1)} %get-tuple-element.66), channel_id=1, source_target_pairs={{0,8},{8,16},{16,24},{1,9},{9,17},{17,25},{2,10},{10,18},{18,26},{... | collective-permute-start | bytes 12296 | tf_op jit(solution)/shard_map/ppermute | solution.py:42
  160.3 1.9 collective-permute-start.4
  162.3 2.9 %collective-permute-done.4 = f32[1,1,8,128]{3,2,1,0:T(8,128)S(1)} collective-permute-done((f32[1,1,8,128]{3,2,1,0:T(8,128)S(1)}, f32[1,1,8,128]{3,2,1,0:T(8,128)S(1)}, u32[]{:S(2)}, u32[]{:S(2)}) %collective-permute-start.4) | collective-permute-done | bytes 4128 | tf_op jit(solution)/shard_map/ppermute | solution.py:43
  165.2 2.7 %collective-permute-start.5 = (f32[1,10,1,128]{3,2,1,0:T(1,128)S(1)}, f32[1,10,1,128]{3,2,1,0:T(1,128)S(1)}, u32[]{:S(2)}, u32[]{:S(2)}) collective-permute-start(f32[1,10,1,128]{3,2,1,0:T(1,128)S(1)} %get-tuple-element.64), channel_id=1, source_target_pairs={{0,1},{1,2},{2,3},{3,4},{4,5},{5,6},{6,7},{8,9},{9,10},{10,11},{11... | collective-permute-start | bytes 15368 | tf_op jit(solution)/shard_map/ppermute | solution.py:42
  169.4 2.9 %collective-permute-done.6 = f32[1,10,1,128]{3,2,1,0:T(1,128)S(1)} collective-permute-done((f32[1,10,1,128]{3,2,1,0:T(1,128)S(1)}, f32[1,10,1,128]{3,2,1,0:T(1,128)S(1)}, u32[]{:S(2)}, u32[]{:S(2)}) %collective-permute-start.6) | collective-permute-done | bytes 5152 | tf_op jit(solution)/shard_map/ppermute | solution.py:43
  172.9 3.4 %collective-permute-start.11 = (f32[5,1,8,128]{3,2,1,0:T(8,128)S(1)}, f32[5,1,8,128]{3,2,1,0:T(8,128)S(1)}, u32[]{:S(2)}, u32[]{:S(2)}) collective-permute-start(f32[5,1,8,128]{3,2,1,0:T(8,128)S(1)} %get-tuple-element.44), channel_id=1, source_target_pairs={{0,8},{8,16},{16,24},{1,9},{9,17},{17,25},{2,10},{10,18},{18,26},{... | collective-permute-start | bytes 61448 | tf_op jit(solution)/shard_map/ppermute | solution.py:42
  176.2 1.9 collective-permute-start.12
  178.2 3.2 %collective-permute-done.12 = f32[5,1,8,128]{3,2,1,0:T(8,128)S(1)} collective-permute-done((f32[5,1,8,128]{3,2,1,0:T(8,128)S(1)}, f32[5,1,8,128]{3,2,1,0:T(8,128)S(1)}, u32[]{:S(2)}, u32[]{:S(2)}) %collective-permute-start.12) | collective-permute-done | bytes 20512 | tf_op jit(solution)/shard_map/ppermute | solution.py:43
  181.4 2.5 %collective-permute-start.13 = (f32[5,10,1,128]{3,2,1,0:T(1,128)S(1)}, f32[5,10,1,128]{3,2,1,0:T(1,128)S(1)}, u32[]{:S(2)}, u32[]{:S(2)}) collective-permute-start(f32[5,10,1,128]{3,2,1,0:T(1,128)S(1)} %get-tuple-element.40), channel_id=1, source_target_pairs={{0,1},{1,2},{2,3},{3,4},{4,5},{5,6},{6,7},{8,9},{9,10},{10,11},{11... | collective-permute-start | bytes 76808 | tf_op jit(solution)/shard_map/ppermute | solution.py:42
  185.3 3.2 %collective-permute-done.14 = f32[5,10,1,128]{3,2,1,0:T(1,128)S(1)} collective-permute-done((f32[5,10,1,128]{3,2,1,0:T(1,128)S(1)}, f32[5,10,1,128]{3,2,1,0:T(1,128)S(1)}, u32[]{:S(2)}, u32[]{:S(2)}) %collective-permute-start.14) | collective-permute-done | bytes 25632 | tf_op jit(solution)/shard_map/ppermute | solution.py:43
  189.0 3.4 %collective-permute-start.15 = (f32[3,1,8,128]{3,2,1,0:T(8,128)S(1)}, f32[3,1,8,128]{3,2,1,0:T(8,128)S(1)}, u32[]{:S(2)}, u32[]{:S(2)}) collective-permute-start(f32[3,1,8,128]{3,2,1,0:T(8,128)S(1)} %get-tuple-element.50), channel_id=1, source_target_pairs={{0,8},{8,16},{16,24},{1,9},{9,17},{17,25},{2,10},{10,18},{18,26},{... | collective-permute-start | bytes 36872 | tf_op jit(solution)/shard_map/ppermute | solution.py:42
  192.3 1.9 collective-permute-start.16
  194.3 3.1 %collective-permute-done.16 = f32[3,1,8,128]{3,2,1,0:T(8,128)S(1)} collective-permute-done((f32[3,1,8,128]{3,2,1,0:T(8,128)S(1)}, f32[3,1,8,128]{3,2,1,0:T(8,128)S(1)}, u32[]{:S(2)}, u32[]{:S(2)}) %collective-permute-start.16) | collective-permute-done | bytes 12320 | tf_op jit(solution)/shard_map/ppermute | solution.py:43
  197.4 2.5 %collective-permute-start.17 = (f32[3,10,1,128]{3,2,1,0:T(1,128)S(1)}, f32[3,10,1,128]{3,2,1,0:T(1,128)S(1)}, u32[]{:S(2)}, u32[]{:S(2)}) collective-permute-start(f32[3,10,1,128]{3,2,1,0:T(1,128)S(1)} %get-tuple-element.46), channel_id=1, source_target_pairs={{0,1},{1,2},{2,3},{3,4},{4,5},{5,6},{6,7},{8,9},{9,10},{10,11},{11... | collective-permute-start | bytes 46088 | tf_op jit(solution)/shard_map/ppermute | solution.py:42
  201.2 3.2 %collective-permute-done.18 = f32[3,10,1,128]{3,2,1,0:T(1,128)S(1)} collective-permute-done((f32[3,10,1,128]{3,2,1,0:T(1,128)S(1)}, f32[3,10,1,128]{3,2,1,0:T(1,128)S(1)}, u32[]{:S(2)}, u32[]{:S(2)}) %collective-permute-start.18) | collective-permute-done | bytes 15392 | tf_op jit(solution)/shard_map/ppermute | solution.py:43
  204.9 3.4 %collective-permute-start.19 = (f32[5,1,8,128]{3,2,1,0:T(8,128)S(1)}, f32[5,1,8,128]{3,2,1,0:T(8,128)S(1)}, u32[]{:S(2)}, u32[]{:S(2)}) collective-permute-start(f32[5,1,8,128]{3,2,1,0:T(8,128)S(1)} %get-tuple-element.42), channel_id=1, source_target_pairs={{0,8},{8,16},{16,24},{1,9},{9,17},{17,25},{2,10},{10,18},{18,26},{... | collective-permute-start | bytes 61448 | tf_op jit(solution)/shard_map/ppermute | solution.py:42
  208.2 1.9 collective-permute-start.20
  210.2 3.2 %collective-permute-done.20 = f32[5,1,8,128]{3,2,1,0:T(8,128)S(1)} collective-permute-done((f32[5,1,8,128]{3,2,1,0:T(8,128)S(1)}, f32[5,1,8,128]{3,2,1,0:T(8,128)S(1)}, u32[]{:S(2)}, u32[]{:S(2)}) %collective-permute-start.20) | collective-permute-done | bytes 20512 | tf_op jit(solution)/shard_map/ppermute | solution.py:43
  213.4 3.7 %collective-permute-start.21 = (f32[5,10,1,128]{3,2,1,0:T(1,128)S(1)}, f32[5,10,1,128]{3,2,1,0:T(1,128)S(1)}, u32[]{:S(2)}, u32[]{:S(2)}) collective-permute-start(f32[5,10,1,128]{3,2,1,0:T(1,128)S(1)} %get-tuple-element.38), channel_id=1, source_target_pairs={{0,1},{1,2},{2,3},{3,4},{4,5},{5,6},{6,7},{8,9},{9,10},{10,11},{11... | collective-permute-start | bytes 76808 | tf_op jit(solution)/shard_map/ppermute | solution.py:42
  218.5 3.1 %collective-permute-done.22 = f32[5,10,1,128]{3,2,1,0:T(1,128)S(1)} collective-permute-done((f32[5,10,1,128]{3,2,1,0:T(1,128)S(1)}, f32[5,10,1,128]{3,2,1,0:T(1,128)S(1)}, u32[]{:S(2)}, u32[]{:S(2)}) %collective-permute-start.22) | collective-permute-done | bytes 25632 | tf_op jit(solution)/shard_map/ppermute | solution.py:43
  (136 shorter events, 20.1 us)
Async XLA Ops:
  0.6 4.5 %copy-start.7 = (s32[256]{0:T(256)S(1)}, s32[256]{0:T(256)}, u32[]{:S(2)}) copy-start(s32[256]{0:T(256)} %param.16) | copy-start | bytes 3076
  6.0 22.6 %collective-permute-start = (f32[1,8,16,2,256]{4,2,3,1,0:T(8,128)S(1)}, f32[1,8,16,2,256]{4,2,3,1,0:T(8,128)S(1)}, u32[]{:S(2)}, u32[]{:S(2)}) collective-permute-start(f32[1,8,16,2,256]{4,2,3,1,0:T(8,128)S(1)} %get-tuple-element.21), channel_id=1, source_target_pairs={{0,8},{8,16},{16,24},{24,0},{1,9},{9,17},{17,25},{25,1},{2,10},{10... | collective-permute-start | bytes 786440 | tf_op jit(solution)/shard_map/ppermute | solution.py:30
  8.6 19.9 %collective-permute-start.1 = (f32[1,8,16,2,256]{4,2,3,1,0:T(8,128)S(1)}, f32[1,8,16,2,256]{4,2,3,1,0:T(8,128)S(1)}, u32[]{:S(2)}, u32[]{:S(2)}) collective-permute-start(f32[1,8,16,2,256]{4,2,3,1,0:T(8,128)S(1)} %get-tuple-element.20), channel_id=1, source_target_pairs={{0,16},{8,24},{16,0},{24,8},{1,17},{9,25},{17,1},{25,9},{2,18},{10... | collective-permute-start | bytes 786440 | tf_op jit(solution)/shard_map/ppermute | solution.py:30
  8.6 19.9 %collective-permute-start.2 = (f32[1,8,16,2,256]{4,2,3,1,0:T(8,128)S(1)}, f32[1,8,16,2,256]{4,2,3,1,0:T(8,128)S(1)}, u32[]{:S(2)}, u32[]{:S(2)}) collective-permute-start(f32[1,8,16,2,256]{4,2,3,1,0:T(8,128)S(1)} %get-tuple-element.19), channel_id=1, source_target_pairs={{0,24},{8,0},{16,8},{24,16},{1,25},{9,1},{17,9},{25,17},{2,26},{10... | collective-permute-start | bytes 786440 | tf_op jit(solution)/shard_map/ppermute | solution.py:30
  10.0 10.3 %all-to-all-start = ((s32[4,1,128]{2,1,0:T(1,128)}), s32[4,1,128]{2,1,0:T(1,128)S(1)}, u32[]{:S(2)}, u32[]{:S(2)}) async-start(s32[4,1,128]{2,1,0:T(1,128)} %reshape.244), calls=%async_computation | async-start | bytes 4096 | tf_op jit(solution)/shard_map/all_to_all | solution.py:215
  22.2 11.7 %all-to-all-start.1 = ((s32[4,8,16]{2,0,1:T(4,128)}), s32[4,8,16]{2,0,1:T(4,128)S(1)}, u32[]{:S(2)}, u32[]{:S(2)}) async-start(s32[4,8,16]{2,0,1:T(4,128)} %copy.41), calls=%async_computation.1 | async-start | bytes 32768 | tf_op jit(solution)/shard_map/all_to_all | solution.py:214
  30.3 7.2 %copy-start = (f32[3,8,8,128]{3,2,1,0:T(8,128)S(1)}, f32[3,8,8,128]{3,2,1,0:T(8,128)}, u32[]{:S(2)}) copy-start(f32[3,8,8,128]{3,2,1,0:T(8,128)} %param.9) | copy-start | bytes 294916
  33.9 27.4 %all-to-all-start.2 = ((f32[4,8,16,2,256]{4,2,3,0,1:T(8,128)}), f32[4,8,16,2,256]{4,2,3,0,1:T(8,128)S(1)}, u32[]{:S(2)}, u32[]{:S(2)}) async-start(f32[4,8,16,2,256]{4,2,3,0,1:T(8,128)} %copy.45), calls=%async_computation.2 | async-start | bytes 2097152 | tf_op jit(solution)/shard_map/all_to_all | solution.py:211
  37.5 7.2 %collective-permute-start.7 = (f32[3,1,8,128]{3,2,1,0:T(8,128)S(1)}, f32[3,1,8,128]{3,2,1,0:T(8,128)S(1)}, u32[]{:S(2)}, u32[]{:S(2)}) collective-permute-start(f32[3,1,8,128]{3,2,1,0:T(8,128)S(1)} %get-tuple-element.53), channel_id=1, source_target_pairs={{0,8},{8,16},{16,24},{1,9},{9,17},{17,25},{2,10},{10,18},{18,26},{... | collective-permute-start | bytes 36872 | tf_op jit(solution)/shard_map/ppermute | solution.py:42
  42.6 5.3 %collective-permute-start.8 = (f32[3,1,8,128]{3,2,1,0:T(8,128)S(1)}, f32[3,1,8,128]{3,2,1,0:T(8,128)S(1)}, u32[]{:S(2)}, u32[]{:S(2)}) collective-permute-start(f32[3,1,8,128]{3,2,1,0:T(8,128)S(1)} %get-tuple-element.52), channel_id=1, source_target_pairs={{8,0},{16,8},{24,16},{9,1},{17,9},{25,17},{10,2},{18,10},{26,18},{... | collective-permute-start | bytes 36872 | tf_op jit(solution)/shard_map/ppermute | solution.py:43
  48.0 114.2 %collective-permute-start.10 = (f32[3,10,1,128]{3,2,1,0:T(1,128)S(1)}, f32[3,10,1,128]{3,2,1,0:T(1,128)S(1)}, u32[]{:S(2)}, u32[]{:S(2)}) collective-permute-start(f32[3,10,1,128]{3,2,1,0:T(1,128)S(1)} %get-tuple-element.49), channel_id=1, source_target_pairs={{1,0},{2,1},{3,2},{4,3},{5,4},{6,5},{7,6},{9,8},{10,9},{11,10},{12... | collective-permute-start | bytes 46088 | tf_op jit(solution)/shard_map/ppermute | solution.py:43
  49.3 113.0 %collective-permute-start.9 = (f32[3,10,1,128]{3,2,1,0:T(1,128)S(1)}, f32[3,10,1,128]{3,2,1,0:T(1,128)S(1)}, u32[]{:S(2)}, u32[]{:S(2)}) collective-permute-start(f32[3,10,1,128]{3,2,1,0:T(1,128)S(1)} %get-tuple-element.48), channel_id=1, source_target_pairs={{0,1},{1,2},{2,3},{3,4},{4,5},{5,6},{6,7},{8,9},{9,10},{10,11},{11... | collective-permute-start | bytes 46088 | tf_op jit(solution)/shard_map/ppermute | solution.py:42
  153.5 18.9 %copy-start.5 = (f32[8,8,128]{2,1,0:T(8,128)S(1)}, f32[8,8,128]{2,1,0:T(8,128)}, u32[]{:S(2)}) copy-start(f32[8,8,128]{2,1,0:T(8,128)} %param.10) | copy-start | bytes 98308
  154.0 18.5 %copy-start.1 = (f32[8,8,128]{2,1,0:T(8,128)}, f32[8,8,128]{2,1,0:T(8,128)S(1)}, u32[]{:S(2)}) copy-start(f32[8,8,128]{2,1,0:T(8,128)S(1)} %fusion.74) | copy-start | bytes 98308
  154.1 8.2 %collective-permute-start.3 = (f32[1,1,8,128]{3,2,1,0:T(8,128)S(1)}, f32[1,1,8,128]{3,2,1,0:T(8,128)S(1)}, u32[]{:S(2)}, u32[]{:S(2)}) collective-permute-start(f32[1,1,8,128]{3,2,1,0:T(8,128)S(1)} %get-tuple-element.66), channel_id=1, source_target_pairs={{0,8},{8,16},{16,24},{1,9},{9,17},{17,25},{2,10},{10,18},{18,26},{... | collective-permute-start | bytes 12296 | tf_op jit(solution)/shard_map/ppermute | solution.py:42
  160.3 4.9 %collective-permute-start.4 = (f32[1,1,8,128]{3,2,1,0:T(8,128)S(1)}, f32[1,1,8,128]{3,2,1,0:T(8,128)S(1)}, u32[]{:S(2)}, u32[]{:S(2)}) collective-permute-start(f32[1,1,8,128]{3,2,1,0:T(8,128)S(1)} %get-tuple-element.67), channel_id=1, source_target_pairs={{8,0},{16,8},{24,16},{9,1},{17,9},{25,17},{10,2},{18,10},{26,18},{... | collective-permute-start | bytes 12296 | tf_op jit(solution)/shard_map/ppermute | solution.py:43
  165.2 4.2 %collective-permute-start.5 = (f32[1,10,1,128]{3,2,1,0:T(1,128)S(1)}, f32[1,10,1,128]{3,2,1,0:T(1,128)S(1)}, u32[]{:S(2)}, u32[]{:S(2)}) collective-permute-start(f32[1,10,1,128]{3,2,1,0:T(1,128)S(1)} %get-tuple-element.64), channel_id=1, source_target_pairs={{0,1},{1,2},{2,3},{3,4},{4,5},{5,6},{6,7},{8,9},{9,10},{10,11},{11... | collective-permute-start | bytes 15368 | tf_op jit(solution)/shard_map/ppermute | solution.py:42
  167.9 4.4 %collective-permute-start.6 = (f32[1,10,1,128]{3,2,1,0:T(1,128)S(1)}, f32[1,10,1,128]{3,2,1,0:T(1,128)S(1)}, u32[]{:S(2)}, u32[]{:S(2)}) collective-permute-start(f32[1,10,1,128]{3,2,1,0:T(1,128)S(1)} %get-tuple-element.65), channel_id=1, source_target_pairs={{1,0},{2,1},{3,2},{4,3},{5,4},{6,5},{7,6},{9,8},{10,9},{11,10},{12... | collective-permute-start | bytes 15368 | tf_op jit(solution)/shard_map/ppermute | solution.py:43
  172.8 15.8 %copy-start.3 = (f32[8,8,128]{2,1,0:T(8,128)S(1)}, f32[8,8,128]{2,1,0:T(8,128)}, u32[]{:S(2)}) copy-start(f32[8,8,128]{2,1,0:T(8,128)} %param.11) | copy-start | bytes 98308
  172.9 5.3 %collective-permute-start.11 = (f32[5,1,8,128]{3,2,1,0:T(8,128)S(1)}, f32[5,1,8,128]{3,2,1,0:T(8,128)S(1)}, u32[]{:S(2)}, u32[]{:S(2)}) collective-permute-start(f32[5,1,8,128]{3,2,1,0:T(8,128)S(1)} %get-tuple-element.44), channel_id=1, source_target_pairs={{0,8},{8,16},{16,24},{1,9},{9,17},{17,25},{2,10},{10,18},{18,26},{... | collective-permute-start | bytes 61448 | tf_op jit(solution)/shard_map/ppermute | solution.py:42
  176.2 5.1 %collective-permute-start.12 = (f32[5,1,8,128]{3,2,1,0:T(8,128)S(1)}, f32[5,1,8,128]{3,2,1,0:T(8,128)S(1)}, u32[]{:S(2)}, u32[]{:S(2)}) collective-permute-start(f32[5,1,8,128]{3,2,1,0:T(8,128)S(1)} %get-tuple-element.45), channel_id=1, source_target_pairs={{8,0},{16,8},{24,16},{9,1},{17,9},{25,17},{10,2},{18,10},{26,18},{... | collective-permute-start | bytes 61448 | tf_op jit(solution)/shard_map/ppermute | solution.py:43
  181.4 3.9 %collective-permute-start.13 = (f32[5,10,1,128]{3,2,1,0:T(1,128)S(1)}, f32[5,10,1,128]{3,2,1,0:T(1,128)S(1)}, u32[]{:S(2)}, u32[]{:S(2)}) collective-permute-start(f32[5,10,1,128]{3,2,1,0:T(1,128)S(1)} %get-tuple-element.40), channel_id=1, source_target_pairs={{0,1},{1,2},{2,3},{3,4},{4,5},{5,6},{6,7},{8,9},{9,10},{10,11},{11... | collective-permute-start | bytes 76808 | tf_op jit(solution)/shard_map/ppermute | solution.py:42
  183.9 4.6 %collective-permute-start.14 = (f32[5,10,1,128]{3,2,1,0:T(1,128)S(1)}, f32[5,10,1,128]{3,2,1,0:T(1,128)S(1)}, u32[]{:S(2)}, u32[]{:S(2)}) collective-permute-start(f32[5,10,1,128]{3,2,1,0:T(1,128)S(1)} %get-tuple-element.41), channel_id=1, source_target_pairs={{1,0},{2,1},{3,2},{4,3},{5,4},{6,5},{7,6},{9,8},{10,9},{11,10},{12... | collective-permute-start | bytes 76808 | tf_op jit(solution)/shard_map/ppermute | solution.py:43
  189.0 5.3 %collective-permute-start.15 = (f32[3,1,8,128]{3,2,1,0:T(8,128)S(1)}, f32[3,1,8,128]{3,2,1,0:T(8,128)S(1)}, u32[]{:S(2)}, u32[]{:S(2)}) collective-permute-start(f32[3,1,8,128]{3,2,1,0:T(8,128)S(1)} %get-tuple-element.50), channel_id=1, source_target_pairs={{0,8},{8,16},{16,24},{1,9},{9,17},{17,25},{2,10},{10,18},{18,26},{... | collective-permute-start | bytes 36872 | tf_op jit(solution)/shard_map/ppermute | solution.py:42
  192.3 5.0 %collective-permute-start.16 = (f32[3,1,8,128]{3,2,1,0:T(8,128)S(1)}, f32[3,1,8,128]{3,2,1,0:T(8,128)S(1)}, u32[]{:S(2)}, u32[]{:S(2)}) collective-permute-start(f32[3,1,8,128]{3,2,1,0:T(8,128)S(1)} %get-tuple-element.51), channel_id=1, source_target_pairs={{8,0},{16,8},{24,16},{9,1},{17,9},{25,17},{10,2},{18,10},{26,18},{... | collective-permute-start | bytes 36872 | tf_op jit(solution)/shard_map/ppermute | solution.py:43
  197.4 3.8 %collective-permute-start.17 = (f32[3,10,1,128]{3,2,1,0:T(1,128)S(1)}, f32[3,10,1,128]{3,2,1,0:T(1,128)S(1)}, u32[]{:S(2)}, u32[]{:S(2)}) collective-permute-start(f32[3,10,1,128]{3,2,1,0:T(1,128)S(1)} %get-tuple-element.46), channel_id=1, source_target_pairs={{0,1},{1,2},{2,3},{3,4},{4,5},{5,6},{6,7},{8,9},{9,10},{10,11},{11... | collective-permute-start | bytes 46088 | tf_op jit(solution)/shard_map/ppermute | solution.py:42
  199.9 4.5 %collective-permute-start.18 = (f32[3,10,1,128]{3,2,1,0:T(1,128)S(1)}, f32[3,10,1,128]{3,2,1,0:T(1,128)S(1)}, u32[]{:S(2)}, u32[]{:S(2)}) collective-permute-start(f32[3,10,1,128]{3,2,1,0:T(1,128)S(1)} %get-tuple-element.47), channel_id=1, source_target_pairs={{1,0},{2,1},{3,2},{4,3},{5,4},{6,5},{7,6},{9,8},{10,9},{11,10},{12... | collective-permute-start | bytes 46088 | tf_op jit(solution)/shard_map/ppermute | solution.py:43
  204.7 17.0 %copy-start.2 = (f32[8,8,128]{2,1,0:T(8,128)}, f32[8,8,128]{2,1,0:T(8,128)S(1)}, u32[]{:S(2)}) copy-start(f32[8,8,128]{2,1,0:T(8,128)S(1)} %get-tuple-element.6) | copy-start | bytes 98308
  204.9 5.3 %collective-permute-start.19 = (f32[5,1,8,128]{3,2,1,0:T(8,128)S(1)}, f32[5,1,8,128]{3,2,1,0:T(8,128)S(1)}, u32[]{:S(2)}, u32[]{:S(2)}) collective-permute-start(f32[5,1,8,128]{3,2,1,0:T(8,128)S(1)} %get-tuple-element.42), channel_id=1, source_target_pairs={{0,8},{8,16},{16,24},{1,9},{9,17},{17,25},{2,10},{10,18},{18,26},{... | collective-permute-start | bytes 61448 | tf_op jit(solution)/shard_map/ppermute | solution.py:42
  208.2 5.1 %collective-permute-start.20 = (f32[5,1,8,128]{3,2,1,0:T(8,128)S(1)}, f32[5,1,8,128]{3,2,1,0:T(8,128)S(1)}, u32[]{:S(2)}, u32[]{:S(2)}) collective-permute-start(f32[5,1,8,128]{3,2,1,0:T(8,128)S(1)} %get-tuple-element.43), channel_id=1, source_target_pairs={{8,0},{16,8},{24,16},{9,1},{17,9},{25,17},{10,2},{18,10},{26,18},{... | collective-permute-start | bytes 61448 | tf_op jit(solution)/shard_map/ppermute | solution.py:43
  213.4 5.1 %collective-permute-start.21 = (f32[5,10,1,128]{3,2,1,0:T(1,128)S(1)}, f32[5,10,1,128]{3,2,1,0:T(1,128)S(1)}, u32[]{:S(2)}, u32[]{:S(2)}) collective-permute-start(f32[5,10,1,128]{3,2,1,0:T(1,128)S(1)} %get-tuple-element.38), channel_id=1, source_target_pairs={{0,1},{1,2},{2,3},{3,4},{4,5},{5,6},{6,7},{8,9},{9,10},{10,11},{11... | collective-permute-start | bytes 76808 | tf_op jit(solution)/shard_map/ppermute | solution.py:42
  217.1 4.6 %collective-permute-start.22 = (f32[5,10,1,128]{3,2,1,0:T(1,128)S(1)}, f32[5,10,1,128]{3,2,1,0:T(1,128)S(1)}, u32[]{:S(2)}, u32[]{:S(2)}) collective-permute-start(f32[5,10,1,128]{3,2,1,0:T(1,128)S(1)} %get-tuple-element.39), channel_id=1, source_target_pairs={{1,0},{2,1},{3,2},{4,3},{5,4},{6,5},{7,6},{9,8},{10,9},{11,10},{12... | collective-permute-start | bytes 76808 | tf_op jit(solution)/shard_map/ppermute | solution.py:43
  (2 other events, 5.2 us)
